TPU v7x, 32 devices: a whole 2x2x4 slice. The times are simulated.
32 devices in a mesh: ctx: 16 (over z, x, core), fsdp: 2 (over y).
Axes of the slice: x: 2, y: 2, z: 4, core: 2. Of those that a mesh axis runs over, the one named last changes fastest.
Arguments:
- block_input: bfloat16 [2, 2048, 2048], P('fsdp', 'ctx'), may hold values from -36 to 36
- query_weight: bfloat16 [2048, 2048], P(('ctx', 'fsdp')), may hold values from -0.125 to 0.125
- key_weight: bfloat16 [2048, 1024], P(('ctx', 'fsdp')), may hold values from -0.125 to 0.125
- value_weight: bfloat16 [2048, 1024], P(('ctx', 'fsdp')), may hold values from -0.125 to 0.125
- output_weight: bfloat16 [2048, 2048], P(('ctx', 'fsdp')), may hold values from -0.375 to 0.375
- gate_weight: bfloat16 [2048, 6144], P(('ctx', 'fsdp')), may hold values from -0.125 to 0.125
- up_weight: bfloat16 [2048, 6144], P(('ctx', 'fsdp')), may hold values from -0.125 to 0.125
- down_weight: bfloat16 [2048, 6144], P(('ctx', 'fsdp')), may hold values from -0.078125 to 0.078125
- attn_gain: float32 [2048], replicated, may hold values from 0.5 to 1.5
- mlp_gain: float32 [2048], replicated, may hold values from 0.5 to 1.5
- query_gain: float32 [128], replicated, may hold values from 0.7 to 2.2
- key_gain: float32 [128], replicated, may hold values from 0.7 to 2.2
- block_order: int32 [32], replicated, may hold values from 0 to 31, each once
- cotangent: bfloat16 [2, 2048, 2048], P('fsdp', 'ctx'), may hold values from -18 to 18
Outputs:
- block_output: bfloat16 [2, 2048, 2048], P('fsdp', 'ctx')
- input_grad: float32 [2, 2048, 2048], P('fsdp', 'ctx')
- query_weight_grad: float32 [2048, 2048], P(('ctx', 'fsdp'))
- key_weight_grad: float32 [2048, 1024], P(('ctx', 'fsdp'))
- value_weight_grad: float32 [2048, 1024], P(('ctx', 'fsdp'))
- output_weight_grad: float32 [2048, 2048], P(('ctx', 'fsdp'))
- gate_weight_grad: float32 [2048, 6144], P(('ctx', 'fsdp'))
- up_weight_grad: float32 [2048, 6144], P(('ctx', 'fsdp'))
- down_weight_grad: float32 [2048, 6144], P(('ctx', 'fsdp'))
- attn_gain_grad: float32 [2048], replicated
- mlp_gain_grad: float32 [2048], replicated
- query_gain_grad: float32 [128], replicated
- key_gain_grad: float32 [128], replicated
Inputs may be any that keep to these rules, and one draw needn't show every extreme that they name: `block_order`: each value appears exactly once.
All inputs are finite; a program needn't handle non-finite values.
Results may differ from a plain program's by a relative error of at most 0.025.
Values may be sent and summed in bfloat16 or wider, within the bound.
No kernel may reach another device: no remote copies, remote signals or barrier semaphores. Data moves between devices by JAX's collectives and lax.ppermute only.
A program may use at most 512 MiB of HBM per device.

v0:
```python
import math
import jax
import jax.numpy as jnp
from jax import lax
from jax.sharding import PartitionSpec as P

eps_model = 1e-06
rope_base = 1000000.0


def inv_root(field):
    return lax.rsqrt(jnp.mean(field * field, axis=-1, keepdims=True) + eps_model)


def norm_back(field, factor, gain, grad_in):
    weighted = gain * grad_in
    inner_mean = jnp.mean(weighted * field, axis=-1, keepdims=True)
    return factor * weighted - field * (factor * factor * factor) * inner_mean


def rope_tables(positions, head_size):
    half_size = head_size // 2
    exponent = jnp.arange(half_size, dtype=jnp.float32) * jnp.float32(2.0 / head_size)
    inverse = jnp.exp(-exponent * jnp.float32(math.log(rope_base)))
    angles = positions.astype(jnp.float32)[:, None] * inverse[None, :]
    return (jnp.cos(angles)[:, None, :], jnp.sin(angles)[:, None, :])


def rotate(field, cosine, sine):
    first_half, second_half = jnp.split(field, 2, axis=-1)
    return jnp.concatenate(
        [first_half * cosine - second_half * sine, second_half * cosine + first_half * sine],
        axis=-1,
    )


def rotate_back(grad_in, cosine, sine):
    first_half, second_half = jnp.split(grad_in, 2, axis=-1)
    return jnp.concatenate(
        [first_half * cosine + second_half * sine, second_half * cosine - first_half * sine],
        axis=-1,
    )


def slot_positions(block_order, first_index, count, half_rows):
    row_index = first_index + jnp.arange(count, dtype=jnp.int32)
    slot_index = row_index // half_rows
    table = jnp.arange(block_order.shape[0], dtype=jnp.int32)
    picked = jnp.sum(
        jnp.where(slot_index[:, None] == table[None, :], block_order[None, :], 0), axis=1
    )
    return picked * half_rows + row_index % half_rows


def outer_rows(left, right):
    return lax.dot_general(
        left, right, (((0,), (0,)), ((), ())), preferred_element_type=jnp.float32
    )


def keep_state(state):
    return state


def stacked_terms(top_left, top_right, low_left, low_right):
    rows = top_left.shape[0]
    left = jnp.concatenate([top_left, low_left], axis=0)
    upper = jnp.concatenate(
        [top_right, jnp.zeros((rows, low_right.shape[1]), top_right.dtype)], axis=1
    )
    lower = jnp.concatenate(
        [jnp.zeros((rows, top_right.shape[1]), low_right.dtype), low_right], axis=1
    )
    return (left, jnp.concatenate([upper, lower], axis=0))


def shards(
    block_input,
    query_weight,
    key_weight,
    value_weight,
    output_weight,
    gate_weight,
    up_weight,
    down_weight,
    attn_gain,
    mlp_gain,
    query_gain,
    key_gain,
    block_order,
    cotangent,
):
    f32 = jnp.float32
    bf16 = jnp.bfloat16
    ctx_size = lax.axis_size("ctx")
    ctx_rank = lax.axis_index("ctx")
    tokens = block_input.shape[1]
    half_rows = tokens // 2
    head_size = query_gain.shape[0]
    heads = query_weight.shape[1] // head_size
    kv_heads = key_weight.shape[1] // head_size
    group = heads // kv_heads
    kv_width = kv_heads * head_size
    hidden_units = gate_weight.shape[1]
    score_scale = 1.0 / math.sqrt(head_size)
    step_cap = max(tokens, 1024)
    forward_weights = (
        lax.all_gather(query_weight, ("ctx", "fsdp"), axis=0, tiled=True),
        lax.all_gather(key_weight, ("ctx", "fsdp"), axis=0, tiled=True),
        lax.all_gather(value_weight, ("ctx", "fsdp"), axis=0, tiled=True),
        lax.all_gather(output_weight, ("ctx", "fsdp"), axis=0, tiled=True),
        lax.all_gather(gate_weight, ("ctx", "fsdp"), axis=0, tiled=True),
        lax.all_gather(up_weight, ("ctx", "fsdp"), axis=0, tiled=True),
        lax.all_gather(down_weight, ("ctx", "fsdp"), axis=0, tiled=True),
    )
    full_query, full_key, full_value, full_output, full_gate, full_up, full_down = forward_weights
    query_pos = slot_positions(block_order, ctx_rank * tokens, tokens, half_rows)
    cosine, sine = rope_tables(query_pos, head_size)
    inputs32 = block_input[0].astype(f32)
    scale_attn = inv_root(inputs32)
    normed_attn = (inputs32 * scale_attn * attn_gain).astype(bf16)
    query_raw = jnp.dot(normed_attn, full_query, preferred_element_type=f32).reshape(
        tokens, heads, head_size
    )
    key_raw = jnp.dot(normed_attn, full_key, preferred_element_type=f32).reshape(
        tokens, kv_heads, head_size
    )
    value_bf = jnp.dot(normed_attn, full_value, preferred_element_type=f32).astype(bf16)
    scale_query = inv_root(query_raw)
    scale_key = inv_root(key_raw)
    query_flat = (
        rotate(query_raw * scale_query * query_gain, cosine, sine)
        .astype(bf16)
        .reshape(tokens, kv_heads, group, head_size)
    )
    query_rot = jnp.transpose(query_flat, (1, 2, 0, 3))
    key_rot = rotate(key_raw * scale_key * key_gain, cosine, sine).astype(bf16)
    keyvals = jnp.concatenate([key_rot.reshape(tokens, kv_width), value_bf], axis=1)

    def attend_block(state, key_block, key_pos):
        weighted_sum, exp_total = state
        block_rows = key_block.shape[0]
        key_heads = key_block[:, :kv_width].reshape(block_rows, kv_heads, head_size)
        value_heads = key_block[:, kv_width:].reshape(block_rows, kv_heads, head_size)
        scores = (
            jnp.einsum("gjqd,kgd->gjqk", query_rot, key_heads, preferred_element_type=f32)
            * score_scale
        )
        allowed = key_pos[None, :] <= query_pos[:, None]
        exp_scores = jnp.where(allowed, jnp.exp(scores), 0.0)
        exp_total = exp_total + jnp.sum(exp_scores, axis=-1)
        weighted_sum = weighted_sum + jnp.einsum(
            "gjqk,kgd->gjqd", exp_scores.astype(bf16), value_heads, preferred_element_type=f32
        )
        return (weighted_sum, exp_total)

    start_sum = jnp.zeros((kv_heads, group, tokens, head_size), f32)
    start_total = jnp.zeros((kv_heads, group, tokens), f32)
    shard_rows = lax.all_gather(keyvals, "ctx", axis=0, tiled=True)
    row_count = shard_rows.shape[0]
    step_rows = math.gcd(row_count, step_cap)

    def turn_step(turn_index, state):
        first_row = turn_index * step_rows
        key_block = lax.dynamic_slice_in_dim(shard_rows, first_row, step_rows, 0)
        key_pos = slot_positions(block_order, first_row, step_rows, half_rows)
        return lax.cond(
            jnp.min(key_pos) <= jnp.max(query_pos),
            lambda inner: attend_block(inner, key_block, key_pos),
            keep_state,
            state,
        )

    weighted_sum, exp_total = lax.fori_loop(
        0, row_count // step_rows, turn_step, (start_sum, start_total)
    )
    attn_heads = weighted_sum / exp_total[..., None]
    attn_four = attn_heads.astype(bf16)
    attn_bf = jnp.transpose(attn_four, (2, 0, 1, 3)).reshape(tokens, heads * head_size)
    log_total = jnp.log(exp_total)
    hidden_one = inputs32 + jnp.einsum(
        "th,dh->td", attn_bf, full_output, preferred_element_type=f32
    )
    scale_mlp = inv_root(hidden_one)
    normed_mlp = (hidden_one * scale_mlp * mlp_gain).astype(bf16)
    gate_pre = jnp.dot(normed_mlp, full_gate, preferred_element_type=f32)
    up_pre = jnp.dot(normed_mlp, full_up, preferred_element_type=f32)
    activated = (jax.nn.silu(gate_pre) * up_pre).astype(bf16)
    block_out = (
        hidden_one + jnp.einsum("tf,df->td", activated, full_down, preferred_element_type=f32)
    ).astype(bf16)
    back_gate, back_up, back_down = (
        lax.all_gather(gate_weight, ("ctx", "fsdp"), axis=0, tiled=True),
        lax.all_gather(up_weight, ("ctx", "fsdp"), axis=0, tiled=True),
        lax.all_gather(down_weight, ("ctx", "fsdp"), axis=0, tiled=True),
    )
    grad_bf = cotangent[0]
    act_grad = jnp.dot(grad_bf, back_down, preferred_element_type=f32)
    sigma = jax.nn.sigmoid(gate_pre)
    gate_grad_in = (act_grad * up_pre * sigma * (1.0 + gate_pre * (1.0 - sigma))).astype(bf16)
    up_grad_in = (act_grad * gate_pre * sigma).astype(bf16)
    normed_mlp_grad = jnp.einsum(
        "tf,df->td", gate_grad_in, back_gate, preferred_element_type=f32
    ) + jnp.einsum("tf,df->td", up_grad_in, back_up, preferred_element_type=f32)
    mlp_gain_part = jnp.sum(normed_mlp_grad * hidden_one * scale_mlp, axis=0)
    hidden_grad = grad_bf.astype(f32) + norm_back(hidden_one, scale_mlp, mlp_gain, normed_mlp_grad)
    hidden_grad_bf = hidden_grad.astype(bf16)
    mlp_left, mlp_right = stacked_terms(
        normed_mlp, jnp.concatenate([gate_grad_in, up_grad_in], axis=1), grad_bf, activated
    )
    mlp_summed = lax.psum_scatter(
        outer_rows(mlp_left, mlp_right), ("ctx", "fsdp"), scatter_dimension=0, tiled=True
    )
    back_query, back_key, back_value, back_output = (
        lax.all_gather(query_weight, ("ctx", "fsdp"), axis=0, tiled=True),
        lax.all_gather(key_weight, ("ctx", "fsdp"), axis=0, tiled=True),
        lax.all_gather(value_weight, ("ctx", "fsdp"), axis=0, tiled=True),
        lax.all_gather(output_weight, ("ctx", "fsdp"), axis=0, tiled=True),
    )
    attn_grad = jnp.dot(hidden_grad_bf, back_output, preferred_element_type=f32).astype(bf16)
    grad_heads = jnp.transpose(attn_grad.reshape(tokens, kv_heads, group, head_size), (1, 2, 0, 3))
    delta_heads = jnp.sum(grad_heads.astype(f32) * attn_four.astype(f32), axis=-1)

    def block_grads(key_block, key_pos, query_grad):
        block_rows = key_block.shape[0]

        def work_block(grad_in):
            key_heads = key_block[:, :kv_width].reshape(block_rows, kv_heads, head_size)
            value_heads = key_block[:, kv_width:].reshape(block_rows, kv_heads, head_size)
            scores = (
                jnp.einsum("gjqd,kgd->gjqk", query_rot, key_heads, preferred_element_type=f32)
                * score_scale
            )
            allowed = key_pos[None, :] <= query_pos[:, None]
            probs = jnp.where(allowed, jnp.exp(scores - log_total[..., None]), 0.0)
            value_part = jnp.einsum(
                "gjqk,gjqd->kgd", probs.astype(bf16), grad_heads, preferred_element_type=f32
            )
            d_probs = jnp.einsum(
                "gjqd,kgd->gjqk", grad_heads, value_heads, preferred_element_type=f32
            )
            d_scores = (probs * (d_probs - delta_heads[..., None])).astype(bf16)
            grad_next = (
                grad_in
                + jnp.einsum("gjqk,kgd->gjqd", d_scores, key_heads, preferred_element_type=f32)
                * score_scale
            )
            key_part = (
                jnp.einsum("gjqk,gjqd->kgd", d_scores, query_rot, preferred_element_type=f32)
                * score_scale
            )
            return (
                grad_next,
                jnp.concatenate(
                    [
                        key_part.reshape(block_rows, kv_width),
                        value_part.reshape(block_rows, kv_width),
                    ],
                    axis=1,
                ),
            )

        def skip_block(grad_in):
            return (grad_in, jnp.zeros((block_rows, 2 * kv_width), f32))

        return lax.cond(jnp.min(key_pos) <= jnp.max(query_pos), work_block, skip_block, query_grad)

    zero_query = jnp.zeros((kv_heads, group, tokens, head_size), f32)
    start_buffer = jnp.zeros((tokens * ctx_size, 2 * kv_width), f32)
    fold_shard_rows = lax.all_gather(keyvals, "ctx", axis=0, tiled=True)
    row_count = fold_shard_rows.shape[0]
    fold_step_rows = math.gcd(row_count, step_cap)

    def turn_step(turn_index, state):
        query_grad, key_buffer = state
        first_row = turn_index * fold_step_rows
        key_block = lax.dynamic_slice_in_dim(fold_shard_rows, first_row, fold_step_rows, 0)
        key_pos = slot_positions(block_order, first_row, fold_step_rows, half_rows)
        query_grad, block_grad = block_grads(key_block, key_pos, query_grad)
        key_buffer = lax.dynamic_update_slice_in_dim(key_buffer, block_grad, first_row, 0)
        return (query_grad, key_buffer)

    query_grad, key_buffer = lax.fori_loop(
        0, row_count // fold_step_rows, turn_step, (zero_query, start_buffer)
    )
    key_grads = lax.psum_scatter(key_buffer, "ctx", scatter_dimension=0, tiled=True)
    query_flat_grad = jnp.transpose(query_grad, (2, 0, 1, 3)).reshape(tokens, heads, head_size)
    query_normed_grad = rotate_back(query_flat_grad, cosine, sine)
    key_normed_grad = rotate_back(
        key_grads[:, :kv_width].reshape(tokens, kv_heads, head_size), cosine, sine
    )
    query_gain_part = jnp.sum(query_normed_grad * query_raw * scale_query, axis=(0, 1))
    key_gain_part = jnp.sum(key_normed_grad * key_raw * scale_key, axis=(0, 1))
    query_pre_grad = (
        norm_back(query_raw, scale_query, query_gain, query_normed_grad)
        .reshape(tokens, heads * head_size)
        .astype(bf16)
    )
    key_pre_grad = (
        norm_back(key_raw, scale_key, key_gain, key_normed_grad)
        .reshape(tokens, kv_width)
        .astype(bf16)
    )
    value_pre_grad = key_grads[:, kv_width:].astype(bf16)
    normed_attn_grad = (
        jnp.einsum("th,dh->td", query_pre_grad, back_query, preferred_element_type=f32)
        + jnp.einsum("th,dh->td", key_pre_grad, back_key, preferred_element_type=f32)
        + jnp.einsum("th,dh->td", value_pre_grad, back_value, preferred_element_type=f32)
    )
    attn_gain_part = jnp.sum(normed_attn_grad * inputs32 * scale_attn, axis=0)
    input_grad = hidden_grad + norm_back(inputs32, scale_attn, attn_gain, normed_attn_grad)
    first_grads = jnp.concatenate([query_pre_grad, key_pre_grad, value_pre_grad], axis=1)
    attn_left, attn_right = stacked_terms(normed_attn, first_grads, hidden_grad_bf, attn_bf)
    attn_summed = lax.psum_scatter(
        outer_rows(attn_left, attn_right), ("ctx", "fsdp"), scatter_dimension=0, tiled=True
    )
    gain_sums = lax.psum(
        (attn_gain_part, mlp_gain_part, query_gain_part, key_gain_part), ("ctx", "fsdp")
    )
    query_cols = heads * head_size
    query_part = attn_summed[:, :query_cols]
    key_part = attn_summed[:, query_cols : query_cols + kv_width]
    value_part = attn_summed[:, query_cols + kv_width : query_cols + 2 * kv_width]
    output_part = attn_summed[:, query_cols + 2 * kv_width :]
    gate_part = mlp_summed[:, :hidden_units]
    up_part = mlp_summed[:, hidden_units : 2 * hidden_units]
    down_part = mlp_summed[:, 2 * hidden_units :]
    return (
        block_out[None],
        input_grad[None],
        query_part,
        key_part,
        value_part,
        output_part,
        gate_part,
        up_part,
        down_part,
        gain_sums[0],
        gain_sums[1],
        gain_sums[2],
        gain_sums[3],
    )


def solution(mesh):
    in_specs = (
        P("fsdp", "ctx", None),
        P(("ctx", "fsdp"), None),
        P(("ctx", "fsdp"), None),
        P(("ctx", "fsdp"), None),
        P(("ctx", "fsdp"), None),
        P(("ctx", "fsdp"), None),
        P(("ctx", "fsdp"), None),
        P(("ctx", "fsdp"), None),
        P(),
        P(),
        P(),
        P(),
        P(),
        P("fsdp", "ctx", None),
    )
    out_specs = (
        P("fsdp", "ctx", None),
        P("fsdp", "ctx", None),
        P(("ctx", "fsdp"), None),
        P(("ctx", "fsdp"), None),
        P(("ctx", "fsdp"), None),
        P(("ctx", "fsdp"), None),
        P(("ctx", "fsdp"), None),
        P(("ctx", "fsdp"), None),
        P(("ctx", "fsdp"), None),
        P(),
        P(),
        P(),
        P(),
    )
    return jax.shard_map(shards, mesh=mesh, in_specs=in_specs, out_specs=out_specs, check_vma=False)
```

profile of v0, /device:TPU:0, one launch (start us, length us, event | category | flops | bytes accessed | tf_op | source)
XLA Modules:
  0.0 2867.1 jit_solution(12603607756975838349)
XLA Ops:
  13.5 62.2 %all-gather.9.cloned.1.call-done = bf16[2048,1024]{1,0:T(8,128)(2,1)} async-done(((bf16[64,1024]{1,0:T(8,128)(2,1)}), bf16[2048,1024]{1,0:T(8,128)(2,1)}) %all-gather.9.cloned.1.call-update) | async-done | bytes 4194320 | tf_op jit(solution)/shard_map/all_gather | solution.py:109
  87.0 52.3 %all-gather.11.cloned.1.call-done = bf16[2048,1024]{1,0:T(8,128)(2,1)} async-done(((bf16[64,1024]{1,0:T(8,128)(2,1)}), bf16[2048,1024]{1,0:T(8,128)(2,1)}) %all-gather.11.cloned.1.call-update) | async-done | bytes 4194320 | tf_op jit(solution)/shard_map/all_gather | solution.py:110
  146.5 71.8 %all-gather.15.cloned.1.call-done = bf16[2048,2048]{1,0:T(8,128)(2,1)} async-done(((bf16[64,2048]{1,0:T(8,128)(2,1)}), bf16[2048,2048]{1,0:T(8,128)(2,1)}) %all-gather.15.cloned.1.call-update) | async-done | bytes 8388624 | tf_op jit(solution)/shard_map/all_gather | solution.py:108
  238.2 56.3 %all-gather.13.cloned.1.call-done = bf16[2048,2048]{1,0:T(8,128)(2,1)} async-done(((bf16[128,2048]{1,0:T(8,128)(2,1)}), bf16[2048,2048]{1,0:T(8,128)(2,1)}) %all-gather.13.cloned.1.call-update) | async-done | bytes 8388624 | tf_op jit(solution)/shard_map/all_gather | solution.py:159
  306.9 19.6 while.37
  327.0 46.1 %all-gather.17.cloned.1.call-done = bf16[2048,2048]{1,0:T(8,128)(2,1)} async-done(((bf16[64,2048]{1,0:T(8,128)(2,1)}), bf16[2048,2048]{1,0:T(8,128)(2,1)}) %all-gather.17.cloned.1.call-update) | async-done | bytes 8388624 | tf_op jit(solution)/shard_map/all_gather | solution.py:111
  379.7 149.4 %all-gather.21.cloned.1.call-done = bf16[2048,6144]{1,0:T(8,128)(2,1)} async-done(((bf16[64,6144]{1,0:T(8,128)(2,1)}), bf16[2048,6144]{1,0:T(8,128)(2,1)}) %all-gather.21.cloned.1.call-update) | async-done | bytes 25165840 | tf_op jit(solution)/shard_map/all_gather | solution.py:113
  529.2 13.2 fusion.114
  542.4 142.5 %all-gather.19.cloned.1.call-done = bf16[2048,6144]{1,0:T(8,128)(2,1)} async-done(((bf16[64,6144]{1,0:T(8,128)(2,1)}), bf16[2048,6144]{1,0:T(8,128)(2,1)}) %all-gather.19.cloned.1.call-update) | async-done | bytes 25165840 | tf_op jit(solution)/shard_map/all_gather | solution.py:112
  684.9 13.2 fusion.113
  698.1 142.5 %all-gather.23.cloned.1.call-done = bf16[2048,6144]{1,0:T(8,128)(2,1)} async-done(((bf16[64,6144]{1,0:T(8,128)(2,1)}), bf16[2048,6144]{1,0:T(8,128)(2,1)}) %all-gather.23.cloned.1.call-update) | async-done | bytes 25165840 | tf_op jit(solution)/shard_map/all_gather | solution.py:114
  840.7 14.9 multiply_convert_fusion
  855.6 14.6 fusion.115
  870.2 14.6 multiply_reduce_fusion.1
  900.3 53.7 %while.38 = (s32[]{:T(128)}, f32[8,2,128,128]{3,2,1,0:T(8,128)S(1)}, f32[2048,2048]{0,1:T(8,128)}, s32[32]{0:T(128)S(1)}, s32[]{:T(128)}, /*index=5*/s32[128]{0:...) while((s32[]{:T(128)}, ...), condition=%wide.region_20.21_spmd, body=%wide.region_15.20_spmd.sunk | while | flops 2709256192 | bytes 99009984 | solution.py:283
  902.5 16.4 conditional.5
  929.2 16.4 conditional.5
  957.6 173.2 %reduce-scatter.4.cloned.1.call-done = f32[128,2048]{0,1:T(8,128)} async-done(((f32[2048,2048]{0,1:T(8,128)}), f32[128,2048]{0,1:T(8,128)}) %reduce-scatter.4.cloned.1.call-update) | async-done | bytes 1048592 | tf_op jit(solution)/shard_map/reduce_scatter | solution.py:286
  1133.5 20.4 fusion.49
  1156.4 79.1 %fusion.37 = f32[2048,18432]{1,0:T(8,128)} fusion(bf16[128,6144]{1,0:T(8,128)(2,1)S(1)} %copy-done.9, bf16[128,6144]{1,0:T(8,128)(2,1)} %broadcast_in_dim.161, bf16[128,6144]{1,0:T(8,128)(2,1)} %get-tuple-element.687, bf16[128,6144]{1,0:T(8,128)(2,1)S(1)} %copy-done.8, bf16[128,2048]{1,0:T(8,128)(2,1)} %bitcast.183, bf16[128,2048]{1,0:T(8,128)(2,1)} %copy-done.10), kind=kOutput, calls=%fused_computation.63 | convolution fusion | flops 19376635904 | bytes 158334976 | tf_op jit(solution)/shard_map/dot_general | solution.py:56
  1244.0 14.1 fusion.61
  1264.4 43.7 %all-reduce.2 = (f32[2048]{0:T(1024)}, f32[2048]{0:T(1024)}, f32[128]{0:T(128)}, f32[128]{0:T(128)}) all-reduce(f32[2048]{0:T(1024)S(1)} %get-tuple-element.627, f32[2048]{0:T(1024)S(1)} %copy-done.38, f32[128]{0:T(128)S(1)} %get-tuple-element.623, f32[128]{0:T(128)S(1)} %get-tuple-element.629), channel_id=1, replica_groups=mesh['ctx'=16,'fsdp'=2] {'ctx','fsdp'}, use_global_device_ids=true, to_apply=%region_28.29 | all-reduce | flops 4352 | bytes 34816 | tf_op jit(solution)/shard_map/psum | solution.py:317
  1309.5 276.1 %reduce-scatter.6.cloned.1.call-done = f32[64,6144]{1,0:T(8,128)} async-done(((f32[2048,6144]{1,0:T(8,128)}), f32[64,6144]{1,0:T(8,128)}) %reduce-scatter.6.cloned.1.call-update) | async-done | bytes 1572880 | tf_op jit(solution)/shard_map/reduce_scatter | solution.py:314
  1589.7 1266.0 %reduce-scatter.8.cloned.1.call-done = f32[64,18432]{1,0:T(8,128)} async-done(((f32[2048,18432]{1,0:T(8,128)}), f32[64,18432]{1,0:T(8,128)}) %reduce-scatter.8.cloned.1.call-update) | async-done | bytes 4718608 | tf_op jit(solution)/shard_map/reduce_scatter | solution.py:211
  (220 shorter events, 195.2 us)
Async XLA Ops:
  7.2 68.5 %all-gather.9.cloned.1.call-start = ((), (), s32[]{:S(2)}) async-start(), calls=%async_computation.3 | async-start | bytes 4325376 | tf_op jit(solution)/shard_map/all_gather | solution.py:109
  7.9 131.3 %all-gather.11.cloned.1.call-start = ((), (), s32[]{:S(2)}) async-start(), calls=%async_computation.4 | async-start | bytes 4325376 | tf_op jit(solution)/shard_map/all_gather | solution.py:110
  8.7 209.7 %all-gather.15.cloned.1.call-start = ((), (), s32[]{:S(2)}) async-start(), calls=%async_computation.6 | async-start | bytes 8650752 | tf_op jit(solution)/shard_map/all_gather | solution.py:108
  9.4 285.1 %all-gather.13.cloned.1.call-start = ((), (), s32[]{:S(2)}) async-start(), calls=%async_computation.5 | async-start | bytes 8912896 | tf_op jit(solution)/shard_map/all_gather | solution.py:159
  12.0 218.7 %copy-start.40 = (f32[128]{0:T(128)}, f32[128]{0:T(128)S(1)}, u32[]{:S(2)}) copy-start(f32[128]{0:T(128)S(1)} %get-tuple-element.712) | copy-start | bytes 1540
  12.2 225.3 %copy-start.25 = (f32[128,64]{0,1:T(8,128)}, f32[128,64]{0,1:T(8,128)S(1)}, u32[]{:S(2)}) copy-start(f32[128,64]{0,1:T(8,128)S(1)} %get-tuple-element.709) | copy-start | bytes 98308
  12.2 225.3 %copy-start.27 = (f32[128,64]{0,1:T(8,128)}, f32[128,64]{0,1:T(8,128)S(1)}, u32[]{:S(2)}) copy-start(f32[128,64]{0,1:T(8,128)S(1)} %get-tuple-element.710) | copy-start | bytes 98308
  13.4 125.8 %copy-start.17 = (bf16[128,2048]{1,0:T(8,128)(2,1)}, bf16[128,2048]{1,0:T(8,128)(2,1)S(1)}, u32[]{:S(2)}) copy-start(bf16[128,2048]{1,0:T(8,128)(2,1)S(1)} %fusion.70) | copy-start | bytes 1572868
  143.0 230.1 %all-gather.17.cloned.1.call-start = ((), (), s32[]{:S(2)}) async-start(), calls=%async_computation.7 | async-start | bytes 8650752 | tf_op jit(solution)/shard_map/all_gather | solution.py:111
  143.6 385.6 %all-gather.21.cloned.1.call-start = ((), (), s32[]{:S(2)}) async-start(), calls=%async_computation.9 | async-start | bytes 25952256 | tf_op jit(solution)/shard_map/all_gather | solution.py:113
  144.2 540.7 %all-gather.19.cloned.1.call-start = ((), (), s32[]{:S(2)}) async-start(), calls=%async_computation.8 | async-start | bytes 25952256 | tf_op jit(solution)/shard_map/all_gather | solution.py:112
  144.9 695.7 %all-gather.23.cloned.1.call-start = ((), (), s32[]{:S(2)}) async-start(), calls=%async_computation.10 | async-start | bytes 25952256 | tf_op jit(solution)/shard_map/all_gather | solution.py:114
  145.7 985.1 %reduce-scatter.4.cloned.1.call-start = ((), (), s32[]{:S(2)}) async-start(), calls=%async_computation.11 | async-start | bytes 17825792 | tf_op jit(solution)/shard_map/reduce_scatter | solution.py:286
  379.5 505.4 %copy-start = (f32[128,2048]{1,0:T(8,128)}, f32[128,2048]{1,0:T(8,128)S(1)}, u32[]{:S(2)}) copy-start(f32[128,2048]{1,0:T(8,128)S(1)} %get-tuple-element.720) | copy-start | bytes 3145732
  379.7 305.2 %copy-start.10 = (bf16[128,2048]{1,0:T(8,128)(2,1)}, bf16[128,2048]{1,0:T(8,128)(2,1)S(1)}, u32[]{:S(2)}) copy-start(bf16[128,2048]{1,0:T(8,128)(2,1)S(1)} %multiply_convert_fusion.3) | copy-start | bytes 1572868
  954.0 631.6 %reduce-scatter.6.cloned.1.call-start = ((), (), s32[]{:S(2)}) async-start(), calls=%async_computation.12 | async-start | bytes 51904512 | tf_op jit(solution)/shard_map/reduce_scatter | solution.py:314
  955.4 176.6 %copy-start.14 = (f32[128,8,128]{0,2,1:T(8,128)S(1)}, f32[128,8,128]{0,2,1:T(8,128)}, u32[]{:S(2)}) copy-start(f32[128,8,128]{0,2,1:T(8,128)} %copy-done.13) | copy-start | bytes 1572868
  955.4 176.6 %copy-start.35 = (f32[128,8]{0,1:T(8,128)S(1)}, f32[128,8]{0,1:T(8,128)}, u32[]{:S(2)}) copy-start(f32[128,8]{0,1:T(8,128)} %copy-done.34) | copy-start | bytes 12292
  955.4 176.6 %copy-start.43 = (f32[128]{0:T(128)S(1)}, f32[128]{0:T(128)}, u32[]{:S(2)}) copy-start(f32[128]{0:T(128)} %param.33) | copy-start | bytes 1540
  956.8 175.4 %copy-start.39 = (f32[128,8]{0,1:T(8,128)S(1)}, f32[128,8]{0,1:T(8,128)}, u32[]{:S(2)}) copy-start(f32[128,8]{0,1:T(8,128)} %get-tuple-element.707) | copy-start | bytes 12292
  957.3 176.2 %copy-start.16 = (bf16[128,2048]{1,0:T(8,128)(2,1)S(1)}, bf16[128,2048]{1,0:T(8,128)(2,1)}, u32[]{:S(2)}) copy-start(bf16[128,2048]{1,0:T(8,128)(2,1)} %copy-done.15) | copy-start | bytes 1572868
  957.3 176.2 %copy-start.18 = (bf16[128,2048]{1,0:T(8,128)(2,1)S(1)}, bf16[128,2048]{1,0:T(8,128)(2,1)}, u32[]{:S(2)}) copy-start(bf16[128,2048]{1,0:T(8,128)(2,1)} %copy-done.17) | copy-start | bytes 1572868
  957.6 196.3 %copy-start.19 = (bf16[128,16,128]{0,2,1:T(8,128)(2,1)}, bf16[128,16,128]{0,2,1:T(8,128)(2,1)S(1)}, u32[]{:S(2)}) copy-start(bf16[128,16,128]{0,2,1:T(8,128)(2,1)S(1)} %subtract_convert_fusion) | copy-start | bytes 1572868
  1154.0 1701.7 %reduce-scatter.8.cloned.1.call-start = ((), (), s32[]{:S(2)}) async-start(), calls=%async_computation.13 | async-start | bytes 155713536 | tf_op jit(solution)/shard_map/reduce_scatter | solution.py:211
  (34 other events, 434.2 us)
Sparse Core Ops, SparseCore 0:
  10.9 64.7 all-gather.8
  78.6 60.6 all-gather.10
  142.4 75.9 all-gather.14
  220.9 73.4 all-gather.12
  297.4 75.6 all-gather.16
  375.9 153.2 all-gather.20
  532.1 152.8 all-gather.18
  687.8 152.8 all-gather.22
  954.1 176.7 reduce-scatter.3
  1154.1 431.4 reduce-scatter.5
  1592.0 1263.6 reduce-scatter.7
where the time goes:
time: 2870 us
  waiting for transfers between devices  2440 us (85%)
  matrix products  249 us (9%)
  local copies, waits for them, and re-layouts  84.8 us (3%)
  blocking collectives  43.7 us (2%)
    reduce_scatter x1, waiting for transfers between devices, shards(): lax.psum_scatter(outer_rows(mlp_left, mlp_right), ('ctx', 'fsdp'), scatte...  1270 us
    reduce_scatter x1, waiting for transfers between devices, shards(): lax.psum_scatter(outer_rows(attn_left, attn_right), ('ctx', 'fsdp'), scat...  276 us
    reduce_scatter x1, waiting for transfers between devices, shards(): lax.psum_scatter(key_buffer, 'ctx', scatter_dimension=0, tiled=True)  173 us
    all_gather x1, waiting for transfers between devices, shards(): lax.all_gather(up_weight, ('ctx', 'fsdp'), axis=0, tiled=True)  149 us
    all_gather x1, waiting for transfers between devices, shards(): lax.all_gather(down_weight, ('ctx', 'fsdp'), axis=0, tiled=True)  143 us
    all_gather x1, waiting for transfers between devices, shards(): lax.all_gather(gate_weight, ('ctx', 'fsdp'), axis=0, tiled=True)  143 us
    dot_general x2, matrix products, outer_rows(): lax.dot_general(left, right, (((0,), (0,)), ((), ())), preferred_element_...  99.6 us
    all_gather x1, waiting for transfers between devices, shards(): lax.all_gather(query_weight, ('ctx', 'fsdp'), axis=0, tiled=True)  71.8 us
  transfers between devices with their start and end apart: 11, of which 11 were waited for; matrix products, arithmetic and copies ran while one was open for 8% of the time, Pallas kernels for 0%

commit v1 on v0

--- a/solution.py
+++ b/solution.py
@@ -6,6 +6,28 @@
 
 eps_model = 1e-06
 rope_base = 1000000.0
+
+
+def joined_along(blocks, dim):
+    blocks = jnp.moveaxis(blocks, 0, dim)
+    dims = blocks.shape
+    return blocks.reshape(*dims[:dim], dims[dim] * dims[dim + 1], *dims[dim + 2 :])
+
+
+def collected_by_bits(x, axis):
+    count = lax.axis_size(axis)
+    blocks = x[None]
+    for level in range(count.bit_length() - 1):
+        bit = 1 << level
+        other = lax.ppermute(blocks, axis, [(i, i ^ bit) for i in range(count)])
+        both = jnp.stack([blocks, other])
+        upper = lax.axis_index(axis) >> level & 1
+        blocks = jnp.where(upper == 0, both, both[::-1]).reshape(-1, *x.shape)
+    return blocks
+
+
+def gather_by_bits(x, axis, dim):
+    return joined_along(collected_by_bits(x, axis), dim)
 
 
 def inv_root(field):
@@ -110,7 +132,7 @@
         lax.all_gather(value_weight, ("ctx", "fsdp"), axis=0, tiled=True),
         lax.all_gather(output_weight, ("ctx", "fsdp"), axis=0, tiled=True),
         lax.all_gather(gate_weight, ("ctx", "fsdp"), axis=0, tiled=True),
-        lax.all_gather(up_weight, ("ctx", "fsdp"), axis=0, tiled=True),
+        gather_by_bits(up_weight, ("ctx", "fsdp"), 0),
         lax.all_gather(down_weight, ("ctx", "fsdp"), axis=0, tiled=True),
     )
     full_query, full_key, full_value, full_output, full_gate, full_up, full_down = forward_weights

time: 2870 us -> 3450 us (1.20)
  waiting for transfers between devices: 2440 us -> 2960 us
  other arithmetic: 25.1 us -> 80.2 us
    ppermute x0 -> x5, waiting for transfers between devices: none -> 929 us  [collected_by_bits(): other = lax.ppermute(blocks, axis, [(i, i ^ bit) for i in range(count)])]
    all_gather x1, waiting for transfers between devices: 143 us -> 0.01 us  [shards(): lax.all_gather(down_weight, ('ctx', 'fsdp'), axis=0, tiled=True)]
    all_gather x1, waiting for transfers between devices: 71.8 us -> 0.01 us  [shards(): lax.all_gather(query_weight, ('ctx', 'fsdp'), axis=0, tiled=True)]
    all_gather x1, waiting for transfers between devices: 143 us -> 83.1 us  [shards(): lax.all_gather(gate_weight, ('ctx', 'fsdp'), axis=0, tiled=True)]
    all_gather x1, waiting for transfers between devices: 56.3 us -> 0.02 us  [shards(): shard_rows = lax.all_gather(keyvals, 'ctx', axis=0, tiled=True)]
    all_gather x1, waiting for transfers between devices: 46.1 us -> 0.02 us  [shards(): lax.all_gather(output_weight, ('ctx', 'fsdp'), axis=0, tiled=True)]
  transfers between devices with their start and end apart: 11 -> 16, of which waited for: 11 -> 12; matrix products, arithmetic and copies ran while one was open for 8% -> 9% of each run, Pallas kernels for 0% -> 0%
where the time goes in v1:
time: 3450 us; the launch traced here: 3440 us
  waiting for transfers between devices  2960 us (86%)
  matrix products  244 us (7%)
  local copies, waits for them, and re-layouts  85.5 us (2%)
  other arithmetic  80.2 us (2%)
  blocking collectives  43.7 us (1%)
    reduce_scatter x1, waiting for transfers between devices, shards(): lax.psum_scatter(outer_rows(mlp_left, mlp_right), ('ctx', 'fsdp'), scatte...  1270 us
    ppermute x5, waiting for transfers between devices, collected_by_bits(): other = lax.ppermute(blocks, axis, [(i, i ^ bit) for i in range(count)])  929 us
    reduce_scatter x1, waiting for transfers between devices, shards(): lax.psum_scatter(outer_rows(attn_left, attn_right), ('ctx', 'fsdp'), scat...  276 us
    reduce_scatter x1, waiting for transfers between devices, shards(): lax.psum_scatter(key_buffer, 'ctx', scatter_dimension=0, tiled=True)  173 us
    all_gather x1, waiting for transfers between devices, shards(): lax.all_gather(up_weight, ('ctx', 'fsdp'), axis=0, tiled=True)  118 us
    dot_general x2, matrix products, outer_rows(): lax.dot_general(left, right, (((0,), (0,)), ((), ())), preferred_element_...  99.6 us
    all_gather x1, waiting for transfers between devices, shards(): lax.all_gather(gate_weight, ('ctx', 'fsdp'), axis=0, tiled=True)  83.1 us
  transfers between devices with their start and end apart: 16, of which 12 were waited for; matrix products, arithmetic and copies ran while one was open for 9% of the time, Pallas kernels for 0%

profile of v1, /device:TPU:0, one launch (start us, length us, event | category | flops | bytes accessed | tf_op | source)
XLA Modules:
  0.0 3443.0 jit_solution(17803438293891015714)
XLA Ops:
  13.6 62.1 %all-gather.9.cloned.1.call-done = bf16[2048,1024]{1,0:T(8,128)(2,1)} async-done(((bf16[64,1024]{1,0:T(8,128)(2,1)}), bf16[2048,1024]{1,0:T(8,128)(2,1)}) %all-gather.9.cloned.1.call-update) | async-done | bytes 4194320 | tf_op jit(solution)/shard_map/all_gather | solution.py:131
  87.3 52.0 %all-gather.11.cloned.1.call-done = bf16[2048,1024]{1,0:T(8,128)(2,1)} async-done(((bf16[64,1024]{1,0:T(8,128)(2,1)}), bf16[2048,1024]{1,0:T(8,128)(2,1)}) %all-gather.11.cloned.1.call-update) | async-done | bytes 4194320 | tf_op jit(solution)/shard_map/all_gather | solution.py:132
  147.3 20.1 collective-permute-done
  178.1 89.8 %collective-permute-done.2 = bf16[4,64,6144]{2,1,0:T(8,128)(2,1)} collective-permute-done((bf16[4,64,6144]{2,1,0:T(8,128)(2,1)}, bf16[4,64,6144]{2,1,0:T(8,128)(2,1)}, u32[]{:S(2)}, u32[]{:S(2)}) %collective-permute-start.2) | collective-permute-done | bytes 3145760 | tf_op jit(solution)/shard_map/ppermute | solution.py:22
  277.3 223.0 %collective-permute-done.3 = bf16[8,64,6144]{2,1,0:T(8,128)(2,1)} collective-permute-done((bf16[8,64,6144]{2,1,0:T(8,128)(2,1)}, bf16[8,64,6144]{2,1,0:T(8,128)(2,1)}, u32[]{:S(2)}, u32[]{:S(2)}) %collective-permute-start.3) | collective-permute-done | bytes 6291488 | tf_op jit(solution)/shard_map/ppermute | solution.py:22
  547.6 19.5 while.37
  575.1 592.0 %collective-permute-done.4 = bf16[16,64,6144]{2,1,0:T(8,128)(2,1)} collective-permute-done((bf16[16,64,6144]{2,1,0:T(8,128)(2,1)}, bf16[16,64,6144]{2,1,0:T(8,128)(2,1)}, u32[]{:S(2)}, u32[]{:S(2)}) %collective-permute-start.4) | collective-permute-done | bytes 12582944 | tf_op jit(solution)/shard_map/ppermute | solution.py:22
  1179.5 13.9 reverse_select_fusion
  1193.4 13.4 fusion.98
  1206.8 83.1 %all-gather.19.cloned.1.call-done = bf16[2048,6144]{1,0:T(8,128)(2,1)} async-done(((bf16[64,6144]{1,0:T(8,128)(2,1)}), bf16[2048,6144]{1,0:T(8,128)(2,1)}) %all-gather.19.cloned.1.call-update) | async-done | bytes 25165840 | tf_op jit(solution)/shard_map/all_gather | solution.py:134
  1300.1 12.5 multiply_convert_fusion
  1312.6 14.7 fusion.116
  1327.3 118.5 %all-gather.23.cloned.1.call-done = bf16[2048,6144]{1,0:T(8,128)(2,1)} async-done(((bf16[64,6144]{1,0:T(8,128)(2,1)}), bf16[2048,6144]{1,0:T(8,128)(2,1)}) %all-gather.23.cloned.1.call-update) | async-done | bytes 25165840 | tf_op jit(solution)/shard_map/all_gather | solution.py:216
  1445.8 14.6 multiply_reduce_fusion.1
  1475.7 53.7 %while.38 = (s32[]{:T(128)}, f32[8,2,128,128]{3,2,1,0:T(8,128)S(1)}, f32[2048,2048]{0,1:T(8,128)}, s32[32]{0:T(128)S(1)}, s32[]{:T(128)}, /*index=5*/s32[128]{0:...) while((s32[]{:T(128)}, ...), condition=%wide.region_20.21_spmd, body=%wide.region_15.20_spmd.sunk | while | flops 2709256192 | bytes 99009984 | solution.py:305
  1478.0 16.4 conditional.5
  1504.7 16.4 conditional.5
  1532.9 173.5 %reduce-scatter.4.cloned.1.call-done = f32[128,2048]{0,1:T(8,128)} async-done(((f32[2048,2048]{0,1:T(8,128)}), f32[128,2048]{0,1:T(8,128)}) %reduce-scatter.4.cloned.1.call-update) | async-done | bytes 1048592 | tf_op jit(solution)/shard_map/reduce_scatter | solution.py:308
  1709.7 20.5 fusion.49
  1732.6 79.1 %fusion.37 = f32[2048,18432]{1,0:T(8,128)} fusion(bf16[128,6144]{1,0:T(8,128)(2,1)S(1)} %copy-done.11, bf16[128,6144]{1,0:T(8,128)(2,1)} %broadcast_in_dim.165, bf16[128,6144]{1,0:T(8,128)(2,1)} %get-tuple-element.687, bf16[128,6144]{1,0:T(8,128)(2,1)S(1)} %copy-done.10, bf16[128,2048]{1,0:T(8,128)(2,1)} %bitcast.193, bf16[128,2048]{1,0:T(8,128)(2,1)} %copy-done.19), kind=kOutput, calls=%fused_computation.68 | convolution fusion | flops 19376635904 | bytes 158334976 | tf_op jit(solution)/shard_map/dot_general | solution.py:78
  1820.2 14.1 fusion.61
  1840.6 43.7 %all-reduce.2 = (f32[2048]{0:T(1024)}, f32[2048]{0:T(1024)}, f32[128]{0:T(128)}, f32[128]{0:T(128)}) all-reduce(f32[2048]{0:T(1024)S(1)} %get-tuple-element.627, f32[2048]{0:T(1024)S(1)} %copy-done.41, f32[128]{0:T(128)S(1)} %get-tuple-element.623, f32[128]{0:T(128)S(1)} %get-tuple-element.629), channel_id=1, replica_groups=mesh['ctx'=16,'fsdp'=2] {'ctx','fsdp'}, use_global_device_ids=true, to_apply=%region_28.29 | all-reduce | flops 4352 | bytes 34816 | tf_op jit(solution)/shard_map/psum | solution.py:339
  1885.6 276.1 %reduce-scatter.6.cloned.1.call-done = f32[64,6144]{1,0:T(8,128)} async-done(((f32[2048,6144]{1,0:T(8,128)}), f32[64,6144]{1,0:T(8,128)}) %reduce-scatter.6.cloned.1.call-update) | async-done | bytes 1572880 | tf_op jit(solution)/shard_map/reduce_scatter | solution.py:336
  2165.8 1265.6 %reduce-scatter.8.cloned.1.call-done = f32[64,18432]{1,0:T(8,128)} async-done(((f32[2048,18432]{1,0:T(8,128)}), f32[64,18432]{1,0:T(8,128)}) %reduce-scatter.8.cloned.1.call-update) | async-done | bytes 4718608 | tf_op jit(solution)/shard_map/reduce_scatter | solution.py:233
  (244 shorter events, 255.4 us)
Async XLA Ops:
  7.2 68.5 %all-gather.9.cloned.1.call-start = ((), (), s32[]{:S(2)}) async-start(), calls=%async_computation.3 | async-start | bytes 4325376 | tf_op jit(solution)/shard_map/all_gather | solution.py:131
  7.9 131.3 %all-gather.11.cloned.1.call-start = ((), (), s32[]{:S(2)}) async-start(), calls=%async_computation.4 | async-start | bytes 4325376 | tf_op jit(solution)/shard_map/all_gather | solution.py:132
  8.7 506.7 %all-gather.15.cloned.1.call-start = ((), (), s32[]{:S(2)}) async-start(), calls=%async_computation.6 | async-start | bytes 8650752 | tf_op jit(solution)/shard_map/all_gather | solution.py:130
  9.4 525.7 %all-gather.13.cloned.1.call-start = ((), (), s32[]{:S(2)}) async-start(), calls=%async_computation.5 | async-start | bytes 8912896 | tf_op jit(solution)/shard_map/all_gather | solution.py:181
  12.1 515.6 %copy-start.43 = (f32[128]{0:T(128)}, f32[128]{0:T(128)S(1)}, u32[]{:S(2)}) copy-start(f32[128]{0:T(128)S(1)} %get-tuple-element.714) | copy-start | bytes 1540
  12.3 522.3 %copy-start.29 = (f32[128,64]{0,1:T(8,128)}, f32[128,64]{0,1:T(8,128)S(1)}, u32[]{:S(2)}) copy-start(f32[128,64]{0,1:T(8,128)S(1)} %get-tuple-element.711) | copy-start | bytes 98308
  12.3 522.2 %copy-start.31 = (f32[128,64]{0,1:T(8,128)}, f32[128,64]{0,1:T(8,128)S(1)}, u32[]{:S(2)}) copy-start(f32[128,64]{0,1:T(8,128)S(1)} %get-tuple-element.712) | copy-start | bytes 98308
  143.0 424.6 %all-gather.17.cloned.1.call-start = ((), (), s32[]{:S(2)}) async-start(), calls=%async_computation.7 | async-start | bytes 8650752 | tf_op jit(solution)/shard_map/all_gather | solution.py:133
  143.6 1049.8 %all-gather.21.cloned.1.call-start = ((), (), s32[]{:S(2)}) async-start(), calls=%async_computation.9 | async-start | bytes 25952256 | tf_op jit(solution)/shard_map/all_gather | solution.py:136
  144.2 1145.8 %all-gather.19.cloned.1.call-start = ((), (), s32[]{:S(2)}) async-start(), calls=%async_computation.8 | async-start | bytes 25952256 | tf_op jit(solution)/shard_map/all_gather | solution.py:134
  144.9 1300.8 %all-gather.23.cloned.1.call-start = ((), (), s32[]{:S(2)}) async-start(), calls=%async_computation.10 | async-start | bytes 25952256 | tf_op jit(solution)/shard_map/all_gather | solution.py:216
  145.7 1560.7 %reduce-scatter.4.cloned.1.call-start = ((), (), s32[]{:S(2)}) async-start(), calls=%async_computation.11 | async-start | bytes 17825792 | tf_op jit(solution)/shard_map/reduce_scatter | solution.py:308
  145.7 21.6 collective-permute-start
  169.1 3.8 collective-permute-start.1
  176.9 91.0 %collective-permute-start.2 = (bf16[4,64,6144]{2,1,0:T(8,128)(2,1)}, bf16[4,64,6144]{2,1,0:T(8,128)(2,1)}, u32[]{:S(2)}, u32[]{:S(2)}) collective-permute-start(bf16[4,64,6144]{2,1,0:T(8,128)(2,1)} %bitcast.40), channel_id=1, source_target_pairs={{0,4},{1,5},{2,6},{3,7},{4,0},{5,1},{6,2},{7,3},{8,12},{9,13},{10,... | collective-permute-start | bytes 9437192 | tf_op jit(solution)/shard_map/ppermute | solution.py:22
  275.6 224.7 %collective-permute-start.3 = (bf16[8,64,6144]{2,1,0:T(8,128)(2,1)}, bf16[8,64,6144]{2,1,0:T(8,128)(2,1)}, u32[]{:S(2)}, u32[]{:S(2)}) collective-permute-start(bf16[8,64,6144]{2,1,0:T(8,128)(2,1)} %bitcast.43), channel_id=1, source_target_pairs={{0,8},{1,9},{2,10},{3,11},{4,12},{5,13},{6,14},{7,15},{8,0},{9,1},... | collective-permute-start | bytes 18874376 | tf_op jit(solution)/shard_map/ppermute | solution.py:22
  514.6 652.4 %collective-permute-start.4 = (bf16[16,64,6144]{2,1,0:T(8,128)(2,1)}, bf16[16,64,6144]{2,1,0:T(8,128)(2,1)}, u32[]{:S(2)}, u32[]{:S(2)}) collective-permute-start(bf16[16,64,6144]{2,1,0:T(8,128)(2,1)} %bitcast.46), channel_id=1, source_target_pairs={{0,16},{1,17},{2,18},{3,19},{4,20},{5,21},{6,22},{7,23},{8,24},{9,... | collective-permute-start | bytes 37748744 | tf_op jit(solution)/shard_map/ppermute | solution.py:22
  574.8 885.5 %copy-start.2 = (f32[128,2048]{1,0:T(8,128)}, f32[128,2048]{1,0:T(8,128)S(1)}, u32[]{:S(2)}) copy-start(f32[128,2048]{1,0:T(8,128)S(1)} %get-tuple-element.722) | copy-start | bytes 3145732
  575.0 714.9 %copy-start.19 = (bf16[128,2048]{1,0:T(8,128)(2,1)}, bf16[128,2048]{1,0:T(8,128)(2,1)S(1)}, u32[]{:S(2)}) copy-start(bf16[128,2048]{1,0:T(8,128)(2,1)S(1)} %multiply_convert_fusion.3) | copy-start | bytes 1572868
  1529.5 632.2 %reduce-scatter.6.cloned.1.call-start = ((), (), s32[]{:S(2)}) async-start(), calls=%async_computation.12 | async-start | bytes 51904512 | tf_op jit(solution)/shard_map/reduce_scatter | solution.py:336
  1530.7 179.0 %copy-start.17 = (bf16[128,2048]{1,0:T(8,128)(2,1)S(1)}, bf16[128,2048]{1,0:T(8,128)(2,1)}, u32[]{:S(2)}) copy-start(bf16[128,2048]{1,0:T(8,128)(2,1)} %copy-done.16) | copy-start | bytes 1572868
  1530.7 179.0 %copy-start.21 = (bf16[128,2048]{1,0:T(8,128)(2,1)S(1)}, bf16[128,2048]{1,0:T(8,128)(2,1)}, u32[]{:S(2)}) copy-start(bf16[128,2048]{1,0:T(8,128)(2,1)} %copy-done.20) | copy-start | bytes 1572868
  1532.9 197.3 %copy-start.22 = (bf16[128,16,128]{0,2,1:T(8,128)(2,1)}, bf16[128,16,128]{0,2,1:T(8,128)(2,1)S(1)}, u32[]{:S(2)}) copy-start(bf16[128,16,128]{0,2,1:T(8,128)(2,1)S(1)} %subtract_convert_fusion) | copy-start | bytes 1572868
  1730.2 1701.2 %reduce-scatter.8.cloned.1.call-start = ((), (), s32[]{:S(2)}) async-start(), calls=%async_computation.13 | async-start | bytes 155713536 | tf_op jit(solution)/shard_map/reduce_scatter | solution.py:233
  (41 other events, 1273.2 us)
Sparse Core Ops, SparseCore 0:
  10.9 64.7 all-gather.8
  78.6 60.6 all-gather.10
  142.4 92.9 all-gather.14
  237.9 98.5 all-gather.12
  339.4 112.3 all-gather.16
  454.6 483.3 all-gather.20
  940.9 349.0 all-gather.18
  1292.8 152.8 all-gather.22
  1529.6 176.7 reduce-scatter.3
  1730.3 431.3 reduce-scatter.5
  2168.1 1263.2 reduce-scatter.7
